TPU v7x, 32 devices: a whole 2x2x4 slice. The times are simulated.
32 devices in a mesh: tm: 8 (over z, x), rows: 4 (over y, core).
Axes of the slice: x: 2, y: 2, z: 4, core: 2. Of those that a mesh axis runs over, the one named last changes fastest.
Arguments:
- observations: float32 [8, 2048], P('tm'), may hold values from -48 to 48
- site_ids: int32 [8, 2048], P('tm'), may hold values from 0 to 4095
- counts: int32 [8], P('tm'), may hold values from 1 to 2048, 12288 in all
- frequencies: float32 [128], replicated, may hold values from -3.140625 to 3.140625
- decay: float32 [128], replicated, may hold values from 0.02 to 0.2
- proc_var: float32 [128], replicated, may hold values from 0.05 to 0.2
Outputs:
- smooth_mean: float32 [8, 256], P('tm', 'rows')
- smooth_cov: float32 [8, 256, 256], P('tm', 'rows')
Inputs may be any that keep to these rules, and one draw needn't show every extreme that they name: Step t observes the sites in its first counts[t] slots; the other slots are ignored.
All inputs are finite; a program needn't handle non-finite values. No bound on the sum of `counts` on one device may be relied on, other than what follows from the above.
Results may differ from a plain program's by a relative error of at most 0.0003.
Values sent between devices are 32-bit elements; how exact they have to be, the bound alone decides.
A program may use at most 128 MiB of HBM per device.

v0:
```python
import functools
import math

import jax
import jax.numpy as jnp
from jax import lax
from jax.experimental import pallas as pl
from jax.experimental.pallas import tpu as pltpu
from jax.sharding import PartitionSpec as P

GRID = 4096
OBS_VAR = 64
TOLERANCE = 3e-5
FINE = 16

exact_mode = lax.Precision.HIGHEST


def exact(left, right):
    return jnp.dot(left, right, precision=exact_mode, preferred_element_type=jnp.float32)


def coarse(left, right):
    return jnp.dot(
        left.astype(jnp.bfloat16), right.astype(jnp.bfloat16), preferred_element_type=jnp.float32
    )


def halves(value):
    high = value.astype(jnp.bfloat16)
    return high, (value - high.astype(jnp.float32)).astype(jnp.bfloat16)


def product(left, right):
    left_high, left_low = left if isinstance(left, tuple) else halves(left)
    right_high, right_low = right if isinstance(right, tuple) else halves(right)
    dot = functools.partial(jnp.dot, preferred_element_type=jnp.float32)
    return dot(left_high, right_high) + (dot(left_high, right_low) + dot(left_low, right_high))


def site_sums(site_row, obs_row, live, modes):
    count = site_row.shape[0]
    weights = (jnp.arange(count, dtype=jnp.int32) < live).astype(jnp.float32)
    groups = 2 * modes // FINE
    steps = jnp.arange(groups, dtype=jnp.int32) * FINE
    exponents = jnp.concatenate(
        [steps - modes, 2 * modes + 1 - steps, steps[: groups // 2] + 1, jnp.arange(FINE)]
    ).astype(jnp.int32)
    phase = (exponents[:, None] * site_row[None, :]) % GRID
    angles = phase.astype(jnp.float32) * (2.0 * math.pi / GRID)
    cosines, sines = jnp.cos(angles), jnp.sin(angles)
    last = exponents.shape[0] - FINE
    scale = jnp.where(jnp.arange(last)[:, None] < 2 * groups, weights[None, :], (weights * obs_row)[None, :])
    left = jnp.concatenate([cosines[:last] * scale, sines[:last] * scale], axis=0)
    right = jnp.concatenate([cosines[last:], sines[last:]], axis=0)
    sums = lax.dot_general(
        left, right, (((1,), (1,)), ((), ())), precision=exact_mode, preferred_element_type=jnp.float32
    )
    cc, cs = sums[:last, :FINE], sums[:last, FINE:]
    sc, ss = sums[last:, :FINE], sums[last:, FINE:]
    one, two = groups, 2 * groups
    near_cos = (cc - ss)[:one].reshape(-1)
    near_sin = (sc + cs)[:one].reshape(-1)
    far_cos = (cc + ss)[one:two].reshape(-1)
    far_sin = (sc - cs)[one:two].reshape(-1)
    info = jnp.concatenate([(cc - ss)[two:].reshape(-1), (sc + cs)[two:].reshape(-1)])
    empty = jnp.zeros_like(info)
    return jnp.stack([near_cos, near_sin, far_cos, far_sin, info, empty, empty, empty])


def invert(sources, splits, targets, low, high):
    width = sources[0].shape[-1]
    rows = lax.broadcasted_iota(jnp.int32, (width, width), 0)
    unit = jnp.where(rows == lax.broadcasted_iota(jnp.int32, (width, width), 1), 1.0, 0.0)
    center = (high + low) / (high - low)
    slope = 2.0 / (high - low)
    top = 2.0 * center * center - 1.0
    for source, split, target in zip(sources, splits, targets):
        matrix = source[...]
        split[0], split[1] = halves(matrix)
        target[...] = (4.0 * center * slope / top) * unit - (2.0 * slope * slope / top) * matrix

    def body(radius):
        factor = 2.0 / (2.0 - radius * radius)
        residues = [
            unit - product((split[0], split[1]), target[...])
            for split, target in zip(splits, targets)
        ]
        for target, residue in zip(targets, residues):
            target[...] = factor * (target[...] + coarse(target[...], residue))
        return radius * radius / (2.0 - radius * radius)

    lax.while_loop(lambda radius: radius > TOLERANCE, body, 1.0 / top)


def solve_kernel(
    where_ref, bounds_ref, sums_ref, turn_ref, turn_cols_ref, damp_ref, damp_cols_ref,
    mean_ref, cov_ref, diag, link, back, info, split, inverse,
):
    steps = sums_ref.shape[0]
    width = sums_ref.shape[2]
    modes = width // 2
    own = where_ref[0]
    block_row = where_ref[1]
    rows = lax.broadcasted_iota(jnp.int32, (width, width), 0)
    cols = lax.broadcasted_iota(jnp.int32, (width, width), 1)
    unit = jnp.where(rows == cols, 1.0, 0.0)
    small_rows = lax.broadcasted_iota(jnp.int32, (modes, modes), 0)
    small_cols = lax.broadcasted_iota(jnp.int32, (modes, modes), 1)
    mirror = jnp.where(small_rows + small_cols == modes - 1, 1.0, 0.0)
    scale = 0.5 / (OBS_VAR * modes)
    info_scale = 1.0 / (OBS_VAR * math.sqrt(modes))
    damp = damp_ref[0:1, :]
    damp_col = damp_cols_ref[:, 0:1]
    wide = damp * damp
    damp_sq = jnp.concatenate([wide, wide], axis=1)

    def shifted(row):
        spread = jnp.broadcast_to(row, (modes, width))
        return pltpu.roll(spread, modes, 1, stride=1, stride_axis=0)[:, :modes]

    most = jnp.zeros((1, width), jnp.float32)
    for step in range(steps):
        near_cos = shifted(sums_ref[step, 0:1, :])
        near_sin = shifted(sums_ref[step, 1:2, :])
        far = jnp.concatenate(
            [shifted(sums_ref[step, 2:3, :]), shifted(sums_ref[step, 3:4, :])], axis=0
        )
        far = exact(far, mirror)
        far_cos, far_sin = far[:modes], far[modes:]
        cosines = turn_ref[step, 0:1, :] * scale
        sines = turn_ref[step, 1:2, :] * scale
        cos_col = turn_cols_ref[step, :, 0:1]
        sin_col = turn_cols_ref[step, :, 1:2]
        up_a, up_b = near_cos + far_cos, far_sin + near_sin
        low_a, low_b = far_sin - near_sin, near_cos - far_cos
        up_left, up_right = up_a * cosines + up_b * sines, up_b * cosines - up_a * sines
        low_left, low_right = low_a * cosines + low_b * sines, low_b * cosines - low_a * sines
        top = jnp.concatenate(
            [cos_col * up_left + sin_col * low_left, cos_col * up_right + sin_col * low_right], axis=1
        )
        bottom = jnp.concatenate(
            [cos_col * low_left - sin_col * up_left, cos_col * low_right - sin_col * up_right], axis=1
        )
        whole = jnp.concatenate([top, bottom], axis=0)
        most = jnp.maximum(most, jnp.sum(jnp.abs(whole), axis=0, keepdims=True))
        edge = 1.0 if step in (0, steps - 1) else 1.0 + damp_sq
        diag[step] = whole + unit * edge
        info_cos, info_sin = sums_ref[step, 4:5, :modes], sums_ref[step, 4:5, modes:]
        turn_cos, turn_sin = turn_ref[step, 0:1, :] * info_scale, turn_ref[step, 1:2, :] * info_scale
        turned = jnp.concatenate(
            [turn_cos * info_cos + turn_sin * info_sin, turn_cos * info_sin - turn_sin * info_cos], axis=1
        )
        info[step] = jnp.broadcast_to(turned, (8, width))
    high = jnp.max(most) + bounds_ref[0]

    def place(position, amount, flipped):
        return jnp.where(flipped, amount - 1 - position, position)

    damp_wide = jnp.concatenate([damp, damp], axis=1)
    damp_tall = jnp.concatenate([damp_col, damp_col], axis=0)
    amount, index, level = steps, own, 0
    base, link_base = 0, 0
    diag_at, link_at = 0, 0
    while amount > 1:
        half = amount // 2
        flipped = lax.rem(index, 2) == 1
        links = amount - 1
        out_base = diag_at + amount
        chunk = min(4, half)
        for start in range(0, half, chunk):
            picks = [diag_at + place(2 * k + 1, amount, flipped) for k in range(start, start + chunk)]
            invert(
                [diag.at[pick] for pick in picks],
                [split.at[k] for k in range(chunk)],
                [inverse.at[k] for k in range(start, start + chunk)],
                bounds_ref[1 + level],
                high,
            )
        for k in range(half):
            kept = diag_at + place(2 * k, amount, flipped)
            diag[out_base + k] = diag[kept]
            info[out_base + k] = info[kept]
        out_links = link_at + (links if level else 0)
        for k in range(half):
            gone = info[diag_at + place(2 * k + 1, amount, flipped)]
            matrix = inverse[k]
            if level == 0:
                moved = damp_tall * matrix * damp_wide
                passed = product(gone * 1.0, matrix) * damp_wide
                diag[out_base + k] -= moved
                info[out_base + k] += passed
                if k + 1 < half:
                    diag[out_base + k + 1] -= moved
                    info[out_base + k + 1] += passed
                    link[out_links + k] = moved
                    back[out_links + k] = moved
                continue
            here = link_at + place(2 * k, links, flipped)
            forth, revert = link[here], back[here]
            forth, revert = jnp.where(flipped, revert, forth), jnp.where(flipped, forth, revert)
            forth, revert, matrix = halves(forth), halves(revert), halves(matrix)
            left = halves(product(matrix, revert))
            diag[out_base + k] -= product(forth, left)
            info[out_base + k] += product(gone, left)
            if k + 1 < half:
                after = link_at + place(2 * k + 1, links, flipped)
                next_forth, next_revert = link[after], back[after]
                next_forth, next_revert = (
                    halves(jnp.where(flipped, next_revert, next_forth)),
                    halves(jnp.where(flipped, next_forth, next_revert)),
                )
                right = halves(product(matrix, next_forth))
                diag[out_base + k + 1] -= product(next_revert, right)
                info[out_base + k + 1] += product(gone, right)
                link[out_links + k] = product(forth, right)
                back[out_links + k] = product(next_revert, left)
        index = place(index, amount, flipped) // 2
        diag_at, link_at = out_base, out_links
        amount, level = half, level + 1

    invert([diag.at[diag_at]], [split.at[0]], [inverse.at[0]], bounds_ref[1 + level], high)
    result = inverse[0]
    state = exact(info[diag_at], result)[0:1]
    cosines, sines = turn_ref[own, 0:1, :], turn_ref[own, 1:2, :]
    cos_col, sin_col = turn_cols_ref[own, :, 0:1], turn_cols_ref[own, :, 1:2]
    left, right = result[:, :modes], result[:, modes:]
    left, right = left * cosines - right * sines, left * sines + right * cosines
    result = jnp.concatenate([left, right], axis=1)
    upper, lower = result[:modes], result[modes:]
    result = jnp.concatenate(
        [cos_col * upper - sin_col * lower, sin_col * upper + cos_col * lower], axis=0
    )
    first, second = state[:, :modes], state[:, modes:]
    state = jnp.concatenate([first * cosines - second * sines, first * sines + second * cosines], axis=1)
    block = cov_ref.shape[0]
    out_rows = lax.broadcasted_iota(jnp.int32, (block, width), 0) + block_row * block
    out_cols = lax.broadcasted_iota(jnp.int32, (block, width), 1)
    pick = jnp.where(out_cols == out_rows // 2 + lax.rem(out_rows, 2) * modes, 1.0, 0.0)
    spread = jnp.where(rows == cols // 2 + lax.rem(cols, 2) * modes, 1.0, 0.0)
    cov_ref[...] = exact(exact(pick, result), spread)
    mean_ref[...] = exact(jnp.broadcast_to(state, (8, width)), spread)


def local(observations, site_ids, counts, frequencies, decay, proc_var):
    modes = frequencies.shape[0]
    width = 2 * modes
    steps = lax.axis_size("tm") * observations.shape[0]
    own = lax.axis_index("tm")
    row_index = lax.axis_index("rows")
    block = width // lax.axis_size("rows")
    sums = site_sums(site_ids[0], observations[0], counts[0], modes)
    sums = lax.all_gather(sums, "tm")
    damping = jnp.exp(-decay)
    root = jnp.sqrt(proc_var)
    times = jnp.arange(steps, dtype=jnp.float32)[:, None]
    turn = jnp.stack([root * jnp.cos(times * frequencies), root * jnp.sin(times * frequencies)], axis=1)
    squared = damping * damping
    levels = (steps - 1).bit_length()
    rest = 1.0 - squared
    bounds = [1.0 + jnp.max(squared)]
    bounds += [jnp.min(rest / (1.0 - jnp.exp(decay * (-2.0 * (1 << level))))) for level in range(levels)]
    bounds += [jnp.min(rest)]
    bounds = jnp.stack(bounds) * jnp.array([1.001] + [0.999] * (levels + 1), jnp.float32)
    damp = jnp.broadcast_to(damping[None, :], (8, modes))
    vmem = pl.BlockSpec(memory_space=pltpu.VMEM)
    smem = pl.BlockSpec(memory_space=pltpu.SMEM)
    mean, cov = pl.pallas_call(
        solve_kernel,
        out_shape=(
            jax.ShapeDtypeStruct((8, width), jnp.float32),
            jax.ShapeDtypeStruct((block, width), jnp.float32),
        ),
        in_specs=[smem, smem, vmem, vmem, vmem, vmem, vmem],
        out_specs=(vmem, vmem),
        scratch_shapes=[
            pltpu.VMEM((2 * steps, width, width), jnp.float32),
            pltpu.VMEM((steps, width, width), jnp.float32),
            pltpu.VMEM((steps, width, width), jnp.float32),
            pltpu.VMEM((2 * steps, 8, width), jnp.float32),
            pltpu.VMEM((4, 2, width, width), jnp.bfloat16),
            pltpu.VMEM((max(1, steps // 2), width, width), jnp.float32),
        ],
        name="solve",
    )(
        jnp.stack([own, row_index]).astype(jnp.int32),
        bounds,
        sums,
        turn,
        jnp.swapaxes(turn, 1, 2),
        damp,
        damp.T,
    )
    mean = lax.dynamic_slice_in_dim(mean[0], row_index * block, block, 0)
    return (mean[None], cov[None])


def solution(mesh):
    return jax.shard_map(
        local,
        mesh=mesh,
        in_specs=(P("tm", None), P("tm", None), P("tm"), P(), P(), P()),
        out_specs=(P("tm", "rows"), P("tm", "rows", None)),
        check_vma=False,
    )
```

profile of v0, /device:TPU:0, one launch (start us, length us, event | category | flops | bytes accessed | tf_op | source)
XLA Modules:
  0.0 67.1 jit_solution(5722162372804246547)
XLA Ops:
  0.6 0.0 copy-start
  0.7 0.1 pad_add_fusion.1
  0.8 0.6 copy-done
  1.3 0.0 copy-start.1
  1.3 1.9 %fusion.11 = (f32[56,2048]{1,0:T(8,128)S(1)}, f32[56,2048]{1,0:T(8,128)S(1)}) fusion(s32[2048]{0:T(1024)S(1)} %bitcast.23, s32[56]{0:T(128)S(1)} %pad_add_fusion.1), kind=kLoop, calls=%fused_computation.18 | loop fusion | flops 1605632 | bytes 925920 | tf_op jit(solution)/shard_map/cos | solution.py:51
  3.8 0.0 copy-done.1
  3.9 0.1 select_multiply_fusion.1
  4.1 0.6 fusion
  4.7 0.1 fusion.18
  4.8 0.1 slice.78
  4.8 0.1 copy.23
  4.9 0.1 reshape.121
  5.0 0.1 slice.79
  5.1 0.1 copy.24
  5.1 0.1 reshape.122
  5.2 0.1 slice_subtract_fusion
  5.3 0.1 copy.22
  5.4 0.1 stack_reshape.15
  5.5 0.1 slice_add_fusion
  5.6 0.1 copy.21
  5.6 0.1 stack_reshape.14
  5.7 0.1 copy.19
  5.8 0.1 stack_reshape.12
  5.9 0.1 copy.20
  5.9 0.1 stack_reshape.13
  6.1 34.4 %all-gather = f32[64,256]{1,0:T(8,128)} all-gather(f32[8,256]{1,0:T(8,128)S(1)} %stack.52), channel_id=2, replica_groups=mesh['tm'=8,'rows'=4] {'tm'}, dimensions={0}, use_global_device_ids=true | all-gather | bytes 73728 | tf_op jit(solution)/shard_map/all_gather | solution.py:253
  40.4 0.0 copy-start.2
  40.4 0.7 copy-done.2
  41.1 0.7 %fusion.17 = (f32[]{:T(128)}, f32[]{:T(128)}, f32[]{:T(128)}, f32[]{:T(128)}, f32[]{:T(128)}, /*index=5*/f32[128]{0:T(128)S(1)}) fusion(f32[128]{0:T(128)S(1)} %copy-done.2), kind=kLoop, calls=%fused_computation.49 | loop fusion | flops 2171 | bytes 1044 | tf_op jit(solution)/shard_map/reduce_min | solution.py:263
  42.4 0.0 copy-start.5
  42.4 2.6 %stack.49 = f32[5]{0:T(128)S(1)} concatenate(f32[1]{0:T(128)} %bitcast.2, f32[1]{0:T(128)} %bitcast.3, f32[1]{0:T(128)} %bitcast.4, f32[1]{0:T(128)} %bitcast.5, f32[1]{0:T(128)} %bitcast.6), dimensions={0} | concatenate | bytes 40 | tf_op jit(solution)/shard_map/stack | solution.py:264
  45.1 0.0 copy-done.5
  45.1 0.5 mul.130.bounds_ref
  45.6 0.7 %transpose.16.damp_cols_ref = f32[128,8]{1,0:T(8,128)} broadcast(f32[128]{0:T(128)S(1)} %get-tuple-element.23), dimensions={0} | broadcast | bytes 4608 | tf_op jit(solution)/shard_map/transpose | solution.py:292
  46.3 0.0 copy-start.4
  46.3 0.6 broadcast_in_dim.49.damp_ref
  46.9 0.1 copy-done.4
  47.0 0.0 copy-start.3
  47.0 0.6 copy-done.3
  47.7 1.0 %copy.25 = f32[8,2,128]{1,2,0:T(8,128)} copy(f32[8,2,128]{2,0,1:T(8,128)S(1)} %pad_maximum_fusion) | data formatting | bytes 16384 | tf_op jit(solution)/shard_map/stack | solution.py:257
  48.7 0.6 copy.26.turn_ref
  49.3 0.6 pad_add_fusion.where_ref
  49.9 15.9 %solve.1 = (f32[8,256]{1,0:T(8,128)}, f32[64,256]{1,0:T(8,128)}) custom-call(s32[2]{0:T(128)} %pad_add_fusion.where_ref, f32[5]{0:T(128)} %mul.130.bounds_ref, f32[8,8,256]{2,1,0:T(8,128)} %bitcast.19, f32[8,2,128]{2,1,0:T(2,128)} %copy.26.turn_ref, f32[8,128,2]{2,1,0:T(8,128)} %bitcast.18, f32[8,128]{1,0:T(8,128)} %broadcast_in_dim.49.damp_ref, ...), custom_call_target="tpu_custom_call" | custom-call | tf_op jit(solution)/shard_map/solve/pallas_call | solution.py:268
  65.8 0.7 %slice.63 = f32[1,256]{1,0:T(1,128)S(1)} slice(f32[8,256]{1,0:T(8,128)} %get-tuple-element.4), slice={[0:1], [0:256]} | slice | bytes 2048 | tf_op jit(solution)/shard_map/slice | solution.py:294
  66.5 0.6 constant_dynamic-slice_fusion
  (16 shorter events, 0.2 us)
Async XLA Ops:
  0.6 0.7 %copy-start = (s32[1,2048]{1,0:T(1,128)S(1)}, s32[1,2048]{1,0:T(1,128)}, u32[]{:S(2)}) copy-start(s32[1,2048]{1,0:T(1,128)} %param.8) | copy-start | bytes 24580
  1.3 2.5 %copy-start.1 = (f32[1,2048]{1,0:T(1,128)S(1)}, f32[1,2048]{1,0:T(1,128)}, u32[]{:S(2)}) copy-start(f32[1,2048]{1,0:T(1,128)} %param.7) | copy-start | bytes 24580
  40.4 0.7 copy-start.2
  42.4 2.6 %copy-start.5 = (f32[5]{0:T(128)S(1)}, f32[5]{0:T(128)}, u32[]{:S(2)}) copy-start(f32[5]{0:T(128)} %constant.62.clone) | copy-start | bytes 64
  46.3 0.7 copy-start.4
  47.0 0.7 copy-start.3
where the time goes:
time: 67.4 us; the launch traced here: 67.1 us
  blocking collectives  34.4 us (51%)
  Pallas kernels  15.9 us (24%)
  local copies, waits for them, and re-layouts  9.89 us (15%)
  other arithmetic  4.2 us (6%)
  between operations  2.08 us (3%)
    all_gather x1, blocking collectives, local(): sums = lax.all_gather(sums, 'tm')  34.4 us
    pallas_call x1, Pallas kernels, local(): pl.pallas_call(solve_kernel, out_shape=(jax.ShapeDtypeStruct((8, width),...  15.9 us
    another operation x1, local copies, waits for them, and re-layouts, local(): jnp.stack(bounds) * jnp.array([1.001] + [0.999] * (levels + 1), jnp.float32)  2.62 us
    unnamed x12, local copies, waits for them, and re-layouts  1.96 us
    cos x1, other arithmetic, site_sums(): cosines, sines = (jnp.cos(angles), jnp.sin(angles))  1.85 us
    another operation x2, local copies, waits for them, and re-layouts, local(): jnp.stack([root * jnp.cos(times * frequencies), root * jnp.sin(times * fr...  1.6 us

commit v1 on v0

--- a/solution.py
+++ b/solution.py
@@ -38,34 +38,133 @@
     return dot(left_high, right_high) + (dot(left_high, right_low) + dot(left_low, right_high))
 
 
-def site_sums(site_row, obs_row, live, modes):
-    count = site_row.shape[0]
-    weights = (jnp.arange(count, dtype=jnp.int32) < live).astype(jnp.float32)
+def parts(value, unit):
+    marked = value * unit
+    off = value - marked
+    column = jnp.sum(marked, axis=1, keepdims=True)
+    row = jnp.sum(marked, axis=0, keepdims=True)
+    return value, off, halves(off), column, row
+
+
+def near(left, right):
+    return product(left[2], right[2]) + left[3] * right[0] + left[1] * right[4]
+
+
+def along(row, right):
+    return product(row, right[2]) + row * right[4]
+
+
+def circle(angle):
+    square = angle * angle
+    cosine = 1.0 / 40320.0 - square * (1.0 / 3628800.0)
+    cosine = 1.0 - square * (0.5 - square * (1.0 / 24.0 - square * (1.0 / 720.0 - square * cosine)))
+    sine = 1.0 / 5040.0 - square * (1.0 / 362880.0)
+    sine = angle * (1.0 - square * (1.0 / 6.0 - square * (1.0 / 120.0 - square * sine)))
+    return cosine, sine
+
+
+def quarter_turn(quadrant, cosine, sine):
+    odd = (quadrant & 1) == 1
+    new_cosine = jnp.where(odd, sine, cosine)
+    new_sine = jnp.where(odd, cosine, sine)
+    new_cosine = jnp.where(((quadrant + 1) & 2) == 2, -new_cosine, new_cosine)
+    new_sine = jnp.where((quadrant & 2) == 2, -new_sine, new_sine)
+    return new_cosine, new_sine
+
+
+def share_kernel(
+    tm_axis, counts_ref, site_ref, obs_ref, freq_ref, decay_ref, var_ref,
+    sums_ref, turn_ref, cols_ref, damp_ref, damp_cols_ref, mine, held, send_sem, recv_sem,
+):
+    count = lax.axis_size(tm_axis)
+    own = lax.axis_index(tm_axis)
+    sites = site_ref.shape[1]
+    modes = freq_ref.shape[1]
+    steps = sums_ref.shape[0]
+    barrier = pltpu.get_barrier_semaphore()
+    for offset in range(1, count):
+        pl.semaphore_signal(
+            barrier, inc=1, device_id={tm_axis: lax.rem(own + offset, count)},
+            device_id_type=pl.DeviceIdType.MESH,
+        )
+
     groups = 2 * modes // FINE
-    steps = jnp.arange(groups, dtype=jnp.int32) * FINE
-    exponents = jnp.concatenate(
-        [steps - modes, 2 * modes + 1 - steps, steps[: groups // 2] + 1, jnp.arange(FINE)]
-    ).astype(jnp.int32)
-    phase = (exponents[:, None] * site_row[None, :]) % GRID
-    angles = phase.astype(jnp.float32) * (2.0 * math.pi / GRID)
-    cosines, sines = jnp.cos(angles), jnp.sin(angles)
-    last = exponents.shape[0] - FINE
-    scale = jnp.where(jnp.arange(last)[:, None] < 2 * groups, weights[None, :], (weights * obs_row)[None, :])
+    total = 2 * groups + groups // 2 + FINE
+    last = total - FINE
+    spot = lax.broadcasted_iota(jnp.int32, (total, sites), 0)
+    exponent = jnp.where(spot < groups, spot * FINE - modes, 2 * modes + 1 - (spot - groups) * FINE)
+    exponent = jnp.where(spot >= 2 * groups, (spot - 2 * groups) * FINE + 1, exponent)
+    exponent = jnp.where(spot >= last, spot - last, exponent)
+    phase = (exponent * site_ref[...]) & (GRID - 1)
+    quadrant = (phase + GRID // 8) >> int(math.log2(GRID // 4))
+    angle = (phase - quadrant * (GRID // 4)).astype(jnp.float32) * (2.0 * math.pi / GRID)
+    cosines, sines = quarter_turn(quadrant, *circle(angle))
+    slots = lax.broadcasted_iota(jnp.int32, (1, sites), 1)
+    weights = jnp.where(slots < counts_ref[0], 1.0, 0.0)
+    scale = jnp.where(spot[:last] < 2 * groups, weights, weights * obs_ref[...])
     left = jnp.concatenate([cosines[:last] * scale, sines[:last] * scale], axis=0)
     right = jnp.concatenate([cosines[last:], sines[last:]], axis=0)
     sums = lax.dot_general(
         left, right, (((1,), (1,)), ((), ())), precision=exact_mode, preferred_element_type=jnp.float32
     )
-    cc, cs = sums[:last, :FINE], sums[:last, FINE:]
-    sc, ss = sums[last:, :FINE], sums[last:, FINE:]
+    wide = lax.broadcasted_iota(jnp.int32, (2 * FINE, 2 * modes), 1)
+    tall = lax.broadcasted_iota(jnp.int32, (2 * FINE, 2 * modes), 0)
+    by_cos = exact(sums, jnp.where(tall == (wide & (FINE - 1)), 1.0, 0.0))
+    by_sin = exact(sums, jnp.where(tall - FINE == (wide & (FINE - 1)), 1.0, 0.0))
     one, two = groups, 2 * groups
-    near_cos = (cc - ss)[:one].reshape(-1)
-    near_sin = (sc + cs)[:one].reshape(-1)
-    far_cos = (cc + ss)[one:two].reshape(-1)
-    far_sin = (sc - cs)[one:two].reshape(-1)
-    info = jnp.concatenate([(cc - ss)[two:].reshape(-1), (sc + cs)[two:].reshape(-1)])
-    empty = jnp.zeros_like(info)
-    return jnp.stack([near_cos, near_sin, far_cos, far_sin, info, empty, empty, empty])
+    cc, cs, sc, ss = by_cos[:last], by_sin[:last], by_cos[last:], by_sin[last:]
+    lane = lax.broadcasted_iota(jnp.int32, (groups, 2 * modes), 1)
+    keep = jnp.where(lane // FINE == lax.broadcasted_iota(jnp.int32, (groups, 2 * modes), 0), 1.0, 0.0)
+
+    def flat(value):
+        return jnp.sum(value * keep[: value.shape[0]], axis=0, keepdims=True)
+
+    near_cos = flat((cc - ss)[:one])
+    near_sin = flat((sc + cs)[:one])
+    far_cos = flat((cc + ss)[one:two])
+    far_sin = flat((sc - cs)[one:two])
+    info = jnp.concatenate([flat((cc - ss)[two:])[:, :modes], flat((sc + cs)[two:])[:, :modes]], axis=1)
+    empty = jnp.zeros((3, 2 * modes), jnp.float32)
+    mine[...] = jnp.concatenate([near_cos, near_sin, far_cos, far_sin, info, empty], axis=0)
+
+    pl.semaphore_wait(barrier, count - 1)
+    copies = []
+    for offset in range(1, count):
+        copy = pltpu.make_async_remote_copy(
+            src_ref=mine,
+            dst_ref=held.at[offset],
+            send_sem=send_sem.at[offset],
+            recv_sem=recv_sem.at[offset],
+            device_id={tm_axis: lax.rem(own + offset, count)},
+            device_id_type=pl.DeviceIdType.MESH,
+        )
+        copy.start()
+        copies.append(copy)
+
+    frequency = freq_ref[...]
+    turns = jnp.where(jnp.abs(frequency) > 0.25 * math.pi, 1, 0) + jnp.where(
+        jnp.abs(frequency) > 0.75 * math.pi, 1, 0
+    )
+    turns = jnp.where(frequency < 0.0, -turns, turns)
+    share = turns.astype(jnp.float32)
+    reduced = (frequency - share * 1.5703125) - share * (0.5 * math.pi - 1.5703125)
+    cosine, sine = quarter_turn(turns + 4, *circle(reduced))
+    damping = jnp.exp(-decay_ref[...])
+    now_cos = jnp.sqrt(var_ref[...])
+    now_sin = jnp.zeros_like(now_cos)
+    for step in range(steps):
+        block = jnp.concatenate([now_cos, now_sin, jnp.zeros((modes - 2, modes), jnp.float32)], axis=0)
+        turn_ref[step] = block[:8]
+        cols_ref[step] = block.T[:, :8]
+        now_cos, now_sin = now_cos * cosine - now_sin * sine, now_cos * sine + now_sin * cosine
+    spread = jnp.broadcast_to(damping, (modes, modes))
+    damp_ref[...] = spread[:8]
+    damp_cols_ref[...] = spread.T[:, :8]
+
+    sums_ref[own] = mine[...]
+    for offset in range(1, count):
+        copies[offset - 1].wait()
+        sums_ref[lax.rem(own + count - offset, count)] = held[offset]
 
 
 def invert(sources, splits, targets, low, high):
@@ -75,17 +174,24 @@
     center = (high + low) / (high - low)
     slope = 2.0 / (high - low)
     top = 2.0 * center * center - 1.0
+    columns = []
     for source, split, target in zip(sources, splits, targets):
         matrix = source[...]
-        split[0], split[1] = halves(matrix)
+        columns.append(jnp.sum(matrix * unit, axis=1, keepdims=True))
+        split[0], split[1] = halves(matrix * (1.0 - unit))
         target[...] = (4.0 * center * slope / top) * unit - (2.0 * slope * slope / top) * matrix
 
     def body(radius):
         factor = 2.0 / (2.0 - radius * radius)
-        residues = [
-            unit - product((split[0], split[1]), target[...])
-            for split, target in zip(splits, targets)
-        ]
+        residues = []
+        for source, split, target, column in zip(sources, splits, targets, columns):
+            marked = target[...] * unit
+            row = jnp.sum(marked, axis=0, keepdims=True)
+            residues.append(
+                (unit - column * target[...])
+                - (source[...] * (1.0 - unit)) * row
+                - product((split[0], split[1]), target[...] - marked)
+            )
         for target, residue in zip(targets, residues):
             target[...] = factor * (target[...] + coarse(target[...], residue))
         return radius * radius / (2.0 - radius * radius)
@@ -94,14 +200,14 @@
 
 
 def solve_kernel(
-    where_ref, bounds_ref, sums_ref, turn_ref, turn_cols_ref, damp_ref, damp_cols_ref,
+    tm_axis, rows_axis, sums_ref, turn_ref, turn_cols_ref, damp_ref, damp_cols_ref,
     mean_ref, cov_ref, diag, link, back, info, split, inverse,
 ):
     steps = sums_ref.shape[0]
     width = sums_ref.shape[2]
     modes = width // 2
-    own = where_ref[0]
-    block_row = where_ref[1]
+    own = lax.axis_index(tm_axis)
+    block_row = lax.axis_index(rows_axis)
     rows = lax.broadcasted_iota(jnp.int32, (width, width), 0)
     cols = lax.broadcasted_iota(jnp.int32, (width, width), 1)
     unit = jnp.where(rows == cols, 1.0, 0.0)
@@ -152,7 +258,10 @@
             [turn_cos * info_cos + turn_sin * info_sin, turn_cos * info_sin - turn_sin * info_cos], axis=1
         )
         info[step] = jnp.broadcast_to(turned, (8, width))
-    high = jnp.max(most) + bounds_ref[0]
+    high = jnp.max(most) * 1.001 + (1.0 + 1.001 * jnp.max(wide))
+
+    def low(power):
+        return 0.999 * jnp.min((1.0 - wide) / (1.0 - power))
 
     def place(position, amount, flipped):
         return jnp.where(flipped, amount - 1 - position, position)
@@ -160,7 +269,7 @@
     damp_wide = jnp.concatenate([damp, damp], axis=1)
     damp_tall = jnp.concatenate([damp_col, damp_col], axis=0)
     amount, index, level = steps, own, 0
-    base, link_base = 0, 0
+    power = wide
     diag_at, link_at = 0, 0
     while amount > 1:
         half = amount // 2
@@ -174,7 +283,7 @@
                 [diag.at[pick] for pick in picks],
                 [split.at[k] for k in range(chunk)],
                 [inverse.at[k] for k in range(start, start + chunk)],
-                bounds_ref[1 + level],
+                low(power),
                 high,
             )
         for k in range(half):
@@ -184,10 +293,10 @@
         out_links = link_at + (links if level else 0)
         for k in range(half):
             gone = info[diag_at + place(2 * k + 1, amount, flipped)]
-            matrix = inverse[k]
+            matrix = parts(inverse[k], unit)
             if level == 0:
-                moved = damp_tall * matrix * damp_wide
-                passed = product(gone * 1.0, matrix) * damp_wide
+                moved = damp_tall * matrix[0] * damp_wide
+                passed = along(gone, matrix) * damp_wide
                 diag[out_base + k] -= moved
                 info[out_base + k] += passed
                 if k + 1 < half:
@@ -199,27 +308,27 @@
             here = link_at + place(2 * k, links, flipped)
             forth, revert = link[here], back[here]
             forth, revert = jnp.where(flipped, revert, forth), jnp.where(flipped, forth, revert)
-            forth, revert, matrix = halves(forth), halves(revert), halves(matrix)
-            left = halves(product(matrix, revert))
-            diag[out_base + k] -= product(forth, left)
-            info[out_base + k] += product(gone, left)
+            forth, revert = parts(forth, unit), parts(revert, unit)
+            left = parts(near(matrix, revert), unit)
+            diag[out_base + k] -= near(forth, left)
+            info[out_base + k] += along(gone, left)
             if k + 1 < half:
                 after = link_at + place(2 * k + 1, links, flipped)
                 next_forth, next_revert = link[after], back[after]
                 next_forth, next_revert = (
-                    halves(jnp.where(flipped, next_revert, next_forth)),
-                    halves(jnp.where(flipped, next_forth, next_revert)),
+                    parts(jnp.where(flipped, next_revert, next_forth), unit),
+                    parts(jnp.where(flipped, next_forth, next_revert), unit),
                 )
-                right = halves(product(matrix, next_forth))
-                diag[out_base + k + 1] -= product(next_revert, right)
-                info[out_base + k + 1] += product(gone, right)
-                link[out_links + k] = product(forth, right)
-                back[out_links + k] = product(next_revert, left)
+                right = parts(near(matrix, next_forth), unit)
+                diag[out_base + k + 1] -= near(next_revert, right)
+                info[out_base + k + 1] += along(gone, right)
+                link[out_links + k] = near(forth, right)
+                back[out_links + k] = near(next_revert, left)
         index = place(index, amount, flipped) // 2
         diag_at, link_at = out_base, out_links
-        amount, level = half, level + 1
-
-    invert([diag.at[diag_at]], [split.at[0]], [inverse.at[0]], bounds_ref[1 + level], high)
+        amount, level, power = half, level + 1, power * power
+
+    invert([diag.at[diag_at]], [split.at[0]], [inverse.at[0]], 0.999 * jnp.min(1.0 - wide), high)
     result = inverse[0]
     state = exact(info[diag_at], result)[0:1]
     cosines, sines = turn_ref[own, 0:1, :], turn_ref[own, 1:2, :]
@@ -233,45 +342,54 @@
     )
     first, second = state[:, :modes], state[:, modes:]
     state = jnp.concatenate([first * cosines - second * sines, first * sines + second * cosines], axis=1)
-    block = cov_ref.shape[0]
+    block = cov_ref.shape[1]
     out_rows = lax.broadcasted_iota(jnp.int32, (block, width), 0) + block_row * block
     out_cols = lax.broadcasted_iota(jnp.int32, (block, width), 1)
     pick = jnp.where(out_cols == out_rows // 2 + lax.rem(out_rows, 2) * modes, 1.0, 0.0)
     spread = jnp.where(rows == cols // 2 + lax.rem(cols, 2) * modes, 1.0, 0.0)
-    cov_ref[...] = exact(exact(pick, result), spread)
-    mean_ref[...] = exact(jnp.broadcast_to(state, (8, width)), spread)
+    cov_ref[0] = exact(exact(pick, result), spread)
+    means = lax.dot_general(
+        jnp.broadcast_to(state, (8, width)), pick, (((1,), (1,)), ((), ())),
+        precision=exact_mode, preferred_element_type=jnp.float32,
+    )
+    mean_ref[...] = means[0:1]
 
 
 def local(observations, site_ids, counts, frequencies, decay, proc_var):
     modes = frequencies.shape[0]
     width = 2 * modes
-    steps = lax.axis_size("tm") * observations.shape[0]
-    own = lax.axis_index("tm")
-    row_index = lax.axis_index("rows")
+    count = lax.axis_size("tm")
+    steps = count * observations.shape[0]
     block = width // lax.axis_size("rows")
-    sums = site_sums(site_ids[0], observations[0], counts[0], modes)
-    sums = lax.all_gather(sums, "tm")
-    damping = jnp.exp(-decay)
-    root = jnp.sqrt(proc_var)
-    times = jnp.arange(steps, dtype=jnp.float32)[:, None]
-    turn = jnp.stack([root * jnp.cos(times * frequencies), root * jnp.sin(times * frequencies)], axis=1)
-    squared = damping * damping
-    levels = (steps - 1).bit_length()
-    rest = 1.0 - squared
-    bounds = [1.0 + jnp.max(squared)]
-    bounds += [jnp.min(rest / (1.0 - jnp.exp(decay * (-2.0 * (1 << level))))) for level in range(levels)]
-    bounds += [jnp.min(rest)]
-    bounds = jnp.stack(bounds) * jnp.array([1.001] + [0.999] * (levels + 1), jnp.float32)
-    damp = jnp.broadcast_to(damping[None, :], (8, modes))
     vmem = pl.BlockSpec(memory_space=pltpu.VMEM)
     smem = pl.BlockSpec(memory_space=pltpu.SMEM)
-    mean, cov = pl.pallas_call(
-        solve_kernel,
+    shared = pl.pallas_call(
+        functools.partial(share_kernel, "tm"),
         out_shape=(
-            jax.ShapeDtypeStruct((8, width), jnp.float32),
-            jax.ShapeDtypeStruct((block, width), jnp.float32),
+            jax.ShapeDtypeStruct((steps, 8, width), jnp.float32),
+            jax.ShapeDtypeStruct((steps, 8, modes), jnp.float32),
+            jax.ShapeDtypeStruct((steps, modes, 8), jnp.float32),
+            jax.ShapeDtypeStruct((8, modes), jnp.float32),
+            jax.ShapeDtypeStruct((modes, 8), jnp.float32),
         ),
-        in_specs=[smem, smem, vmem, vmem, vmem, vmem, vmem],
+        in_specs=[smem] + [vmem] * 5,
+        out_specs=(vmem,) * 5,
+        scratch_shapes=[
+            pltpu.VMEM((8, width), jnp.float32),
+            pltpu.VMEM((count, 8, width), jnp.float32),
+            pltpu.SemaphoreType.DMA((count,)),
+            pltpu.SemaphoreType.DMA((count,)),
+        ],
+        compiler_params=pltpu.CompilerParams(collective_id=0, has_side_effects=True),
+        name="share",
+    )(counts, site_ids, observations, frequencies[None], decay[None], proc_var[None])
+    return pl.pallas_call(
+        functools.partial(solve_kernel, "tm", "rows"),
+        out_shape=(
+            jax.ShapeDtypeStruct((1, block), jnp.float32),
+            jax.ShapeDtypeStruct((1, block, width), jnp.float32),
+        ),
+        in_specs=[vmem] * 5,
         out_specs=(vmem, vmem),
         scratch_shapes=[
             pltpu.VMEM((2 * steps, width, width), jnp.float32),
@@ -282,17 +400,7 @@
             pltpu.VMEM((max(1, steps // 2), width, width), jnp.float32),
         ],
         name="solve",
-    )(
-        jnp.stack([own, row_index]).astype(jnp.int32),
-        bounds,
-        sums,
-        turn,
-        jnp.swapaxes(turn, 1, 2),
-        damp,
-        damp.T,
-    )
-    mean = lax.dynamic_slice_in_dim(mean[0], row_index * block, block, 0)
-    return (mean[None], cov[None])
+    )(*shared)
 
 
 def solution(mesh):

time: 67.4 us -> 29.2 us (0.43)
  blocking collectives: 34.4 us -> 0 us
  Pallas kernels: 15.9 us -> 27.7 us
  local copies, waits for them, and re-layouts: 9.89 us -> 0 us
  other arithmetic: 4.2 us -> 0 us
  between operations: 2.08 us -> 1.28 us
    all_gather x1 -> x0, blocking collectives: 34.4 us -> none  [local(): sums = lax.all_gather(sums, 'tm')]
    pallas_call x1 -> x2, Pallas kernels: 15.9 us -> 27.7 us  [the longest x1 16.8 us: local(): pl.pallas_call(functools.partial(solve_kernel, 'tm', 'rows'), out_shape=(...]
    another operation x10 -> x0, local copies, waits for them, and re-layouts: 4.6 us -> none  [the longest x1 2.62 us: local(): jnp.stack(bounds) * jnp.array([1.001] + [0.999] * (levels + 1), jnp.float32)]
    unnamed x12 -> x0, local copies, waits for them, and re-layouts: 1.96 us -> none
    cos x1 -> x0, other arithmetic: 1.85 us -> none  [site_sums(): cosines, sines = (jnp.cos(angles), jnp.sin(angles))]
    slice x11 -> x0, local copies, waits for them, and re-layouts: 1.29 us -> none  [the longest x1 0.7 us: local(): mean = lax.dynamic_slice_in_dim(mean[0], row_index * block, block, 0)]
    mul x5 -> x0, other arithmetic: 0.73 us -> none  [the longest x1 0.55 us: local(): jnp.stack(bounds) * jnp.array([1.001] + [0.999] * (levels + 1), jnp.float32)]
    transpose x1 -> x0, local copies, waits for them, and re-layouts: 0.7 us -> none  [local(): mean, cov = pl.pallas_call(solve_kernel, out_shape=(jax.ShapeDtypeStruct(...]
where the time goes in v1:
time: 29.2 us; the launch traced here: 29 us
  Pallas kernels  27.7 us (95%)
  between operations  1.28 us (4%)
    pallas_call x1, Pallas kernels, local(): pl.pallas_call(functools.partial(solve_kernel, 'tm', 'rows'), out_shape=(...  16.8 us
    pallas_call x1, Pallas kernels, local(): pl.pallas_call(functools.partial(share_kernel, 'tm'), out_shape=(jax.Shap...  11 us

profile of v1, /device:TPU:0, one launch (start us, length us, event | category | flops | bytes accessed | tf_op | source)
XLA Modules:
  0.0 29.0 jit_solution(15994606367659687021)
XLA Ops:
  1.3 11.0 %share.1 = (f32[8,8,256]{2,1,0:T(8,128)}, f32[8,8,128]{2,1,0:T(8,128)}, f32[8,128,8]{2,1,0:T(8,128)}, f32[8,128]{1,0:T(8,128)}, f32[128,8]{1,0:T(8,128)}) custom-call(s32[1]{0:T(128)S(6)} %copy.8.counts_ref, s32[1,2048]{1,0:T(1,128)} %site_ref.1, f32[1,2048]{1,0:T(1,128)} %obs_ref.1, f32[1,128]{1,0:T(1,128)} %bitcast.3, f32[1,128]{1,0:T(1,128)} %bitcast.4, ...), custom_call_target="tpu_custom_call" | custom-call | tf_op jit(solution)/shard_map/share/pallas_call | solution.py:366
  12.3 16.8 %solve.1 = (f32[1,64]{1,0:T(1,128)}, f32[1,64,256]{2,1,0:T(8,128)}) custom-call(f32[8,8,256]{2,1,0:T(8,128)} %get-tuple-element.7.sums_ref, f32[8,8,128]{2,1,0:T(8,128)} %get-tuple-element.8.turn_ref, f32[8,128,8]{2,1,0:T(8,128)} %get-tuple-element.9.turn_cols_ref, f32[8,128]{1,0:T(8,128)} %get-tuple-element.10.damp_ref, ...), custom_call_target="tpu_custom_call" | custom-call | tf_op jit(solution)/shard_map/solve/pallas_call | solution.py:386

commit v2 on v1

--- a/solution.py
+++ b/solution.py
@@ -11,6 +11,7 @@
 GRID = 4096
 OBS_VAR = 64
 TOLERANCE = 3e-5
+INNER_TOLERANCE = 4e-6
 FINE = 16
 
 exact_mode = lax.Precision.HIGHEST
@@ -36,6 +37,20 @@
     right_high, right_low = right if isinstance(right, tuple) else halves(right)
     dot = functools.partial(jnp.dot, preferred_element_type=jnp.float32)
     return dot(left_high, right_high) + (dot(left_high, right_low) + dot(left_low, right_high))
+
+
+def spread_by(value, picks):
+    high, low = halves(value)
+    picks = picks.astype(jnp.bfloat16)
+    dot = functools.partial(jnp.dot, preferred_element_type=jnp.float32)
+    return dot(high, picks) + dot(low, picks)
+
+
+def picked_by(picks, value):
+    high, low = halves(value)
+    picks = picks.astype(jnp.bfloat16)
+    dot = functools.partial(jnp.dot, preferred_element_type=jnp.float32)
+    return dot(picks, high) + dot(picks, low)
 
 
 def parts(value, unit):
@@ -104,13 +119,18 @@
     scale = jnp.where(spot[:last] < 2 * groups, weights, weights * obs_ref[...])
     left = jnp.concatenate([cosines[:last] * scale, sines[:last] * scale], axis=0)
     right = jnp.concatenate([cosines[last:], sines[last:]], axis=0)
-    sums = lax.dot_general(
-        left, right, (((1,), (1,)), ((), ())), precision=exact_mode, preferred_element_type=jnp.float32
-    )
+    left_high, left_low = halves(left)
+    right_high, right_low = halves(right)
+    beside = functools.partial(
+        lax.dot_general,
+        dimension_numbers=(((1,), (1,)), ((), ())),
+        preferred_element_type=jnp.float32,
+    )
+    sums = beside(left_high, right_high) + (beside(left_high, right_low) + beside(left_low, right_high))
     wide = lax.broadcasted_iota(jnp.int32, (2 * FINE, 2 * modes), 1)
     tall = lax.broadcasted_iota(jnp.int32, (2 * FINE, 2 * modes), 0)
-    by_cos = exact(sums, jnp.where(tall == (wide & (FINE - 1)), 1.0, 0.0))
-    by_sin = exact(sums, jnp.where(tall - FINE == (wide & (FINE - 1)), 1.0, 0.0))
+    by_cos = spread_by(sums, jnp.where(tall == (wide & (FINE - 1)), 1.0, 0.0))
+    by_sin = spread_by(sums, jnp.where(tall - FINE == (wide & (FINE - 1)), 1.0, 0.0))
     one, two = groups, 2 * groups
     cc, cs, sc, ss = by_cos[:last], by_sin[:last], by_cos[last:], by_sin[last:]
     lane = lax.broadcasted_iota(jnp.int32, (groups, 2 * modes), 1)
@@ -167,41 +187,60 @@
         sums_ref[lax.rem(own + count - offset, count)] = held[offset]
 
 
-def invert(sources, splits, targets, low, high):
+def invert(sources, targets, low, high, tolerance):
     width = sources[0].shape[-1]
     rows = lax.broadcasted_iota(jnp.int32, (width, width), 0)
     unit = jnp.where(rows == lax.broadcasted_iota(jnp.int32, (width, width), 1), 1.0, 0.0)
     center = (high + low) / (high - low)
     slope = 2.0 / (high - low)
     top = 2.0 * center * center - 1.0
-    columns = []
-    for source, split, target in zip(sources, splits, targets):
+    scaled = []
+    bound = 0.0
+    for source in sources:
         matrix = source[...]
-        columns.append(jnp.sum(matrix * unit, axis=1, keepdims=True))
-        split[0], split[1] = halves(matrix * (1.0 - unit))
-        target[...] = (4.0 * center * slope / top) * unit - (2.0 * slope * slope / top) * matrix
+        marked = matrix * unit
+        tall = lax.rsqrt(jnp.sum(marked, axis=1, keepdims=True))
+        wide = lax.rsqrt(jnp.sum(marked, axis=0, keepdims=True))
+        off = (matrix - marked) * tall * wide
+        parted = halves(off)
+        square = product(parted, parted)
+        bound = jnp.maximum(bound, jnp.max(jnp.sum(jnp.abs(square), axis=0, keepdims=True)))
+        scaled.append((tall, wide, off, parted[0], square))
+    good = bound < 0.81
+    bound = jnp.minimum(bound * 1.001, 0.81)
+    start = bound / (2.0 - bound)
+    gain = 4.0 / ((2.0 - start * start) * (2.0 - bound))
+    for source, target, (tall, wide, off, high_off, square) in zip(sources, targets, scaled):
+        residue = (2.0 * square - bound * unit) * (1.0 / (2.0 - bound))
+        moved = jnp.dot(high_off, residue.astype(jnp.bfloat16), preferred_element_type=jnp.float32)
+        taken = gain * (unit - off + residue - moved) * tall * wide
+        other = (4.0 * center * slope / top) * unit - (2.0 * slope * slope / top) * source[...]
+        target[...] = jnp.where(good, taken, other)
 
     def body(radius):
         factor = 2.0 / (2.0 - radius * radius)
         residues = []
-        for source, split, target, column in zip(sources, splits, targets, columns):
+        for source, target in zip(sources, targets):
             marked = target[...] * unit
             row = jnp.sum(marked, axis=0, keepdims=True)
+            matrix = source[...]
+            base = matrix * unit
+            off = matrix - base
+            column = jnp.sum(base, axis=1, keepdims=True)
             residues.append(
-                (unit - column * target[...])
-                - (source[...] * (1.0 - unit)) * row
-                - product((split[0], split[1]), target[...] - marked)
+                (unit - column * target[...]) - off * row - product(halves(off), target[...] - marked)
             )
         for target, residue in zip(targets, residues):
             target[...] = factor * (target[...] + coarse(target[...], residue))
         return radius * radius / (2.0 - radius * radius)
 
-    lax.while_loop(lambda radius: radius > TOLERANCE, body, 1.0 / top)
+    first = jnp.where(good, start * start / (2.0 - start * start), 1.0 / top)
+    lax.while_loop(lambda radius: radius > tolerance, body, first)
 
 
 def solve_kernel(
     tm_axis, rows_axis, sums_ref, turn_ref, turn_cols_ref, damp_ref, damp_cols_ref,
-    mean_ref, cov_ref, diag, link, back, info, split, inverse,
+    mean_ref, cov_ref, diag, link, back, info, inverse,
 ):
     steps = sums_ref.shape[0]
     width = sums_ref.shape[2]
@@ -226,14 +265,17 @@
         return pltpu.roll(spread, modes, 1, stride=1, stride_axis=0)[:, :modes]
 
     most = jnp.zeros((1, width), jnp.float32)
+    far_all = spread_by(
+        jnp.concatenate(
+            [shifted(sums_ref[step, row : row + 1, :]) for step in range(steps) for row in (2, 3)], axis=0
+        ),
+        mirror,
+    )
     for step in range(steps):
         near_cos = shifted(sums_ref[step, 0:1, :])
         near_sin = shifted(sums_ref[step, 1:2, :])
-        far = jnp.concatenate(
-            [shifted(sums_ref[step, 2:3, :]), shifted(sums_ref[step, 3:4, :])], axis=0
-        )
-        far = exact(far, mirror)
-        far_cos, far_sin = far[:modes], far[modes:]
+        far_cos = far_all[2 * step * modes : (2 * step + 1) * modes]
+        far_sin = far_all[(2 * step + 1) * modes : (2 * step + 2) * modes]
         cosines = turn_ref[step, 0:1, :] * scale
         sines = turn_ref[step, 1:2, :] * scale
         cos_col = turn_cols_ref[step, :, 0:1]
@@ -281,10 +323,10 @@
             picks = [diag_at + place(2 * k + 1, amount, flipped) for k in range(start, start + chunk)]
             invert(
                 [diag.at[pick] for pick in picks],
-                [split.at[k] for k in range(chunk)],
                 [inverse.at[k] for k in range(start, start + chunk)],
                 low(power),
                 high,
+                INNER_TOLERANCE,
             )
         for k in range(half):
             kept = diag_at + place(2 * k, amount, flipped)
@@ -303,22 +345,29 @@
                     diag[out_base + k + 1] -= moved
                     info[out_base + k + 1] += passed
                     link[out_links + k] = moved
-                    back[out_links + k] = moved
                 continue
             here = link_at + place(2 * k, links, flipped)
-            forth, revert = link[here], back[here]
-            forth, revert = jnp.where(flipped, revert, forth), jnp.where(flipped, forth, revert)
-            forth, revert = parts(forth, unit), parts(revert, unit)
+            if level == 1:
+                forth = revert = parts(link[here], unit)
+            else:
+                forth, revert = link[here], back[here]
+                forth, revert = (
+                    parts(jnp.where(flipped, revert, forth), unit),
+                    parts(jnp.where(flipped, forth, revert), unit),
+                )
             left = parts(near(matrix, revert), unit)
             diag[out_base + k] -= near(forth, left)
             info[out_base + k] += along(gone, left)
             if k + 1 < half:
                 after = link_at + place(2 * k + 1, links, flipped)
-                next_forth, next_revert = link[after], back[after]
-                next_forth, next_revert = (
-                    parts(jnp.where(flipped, next_revert, next_forth), unit),
-                    parts(jnp.where(flipped, next_forth, next_revert), unit),
-                )
+                if level == 1:
+                    next_forth = next_revert = parts(link[after], unit)
+                else:
+                    next_forth, next_revert = link[after], back[after]
+                    next_forth, next_revert = (
+                        parts(jnp.where(flipped, next_revert, next_forth), unit),
+                        parts(jnp.where(flipped, next_forth, next_revert), unit),
+                    )
                 right = parts(near(matrix, next_forth), unit)
                 diag[out_base + k + 1] -= near(next_revert, right)
                 info[out_base + k + 1] += along(gone, right)
@@ -328,9 +377,9 @@
         diag_at, link_at = out_base, out_links
         amount, level, power = half, level + 1, power * power
 
-    invert([diag.at[diag_at]], [split.at[0]], [inverse.at[0]], 0.999 * jnp.min(1.0 - wide), high)
+    invert([diag.at[diag_at]], [inverse.at[0]], 0.999 * jnp.min(1.0 - wide), high, TOLERANCE)
     result = inverse[0]
-    state = exact(info[diag_at], result)[0:1]
+    state = along(info[diag_at], parts(result, unit))[0:1]
     cosines, sines = turn_ref[own, 0:1, :], turn_ref[own, 1:2, :]
     cos_col, sin_col = turn_cols_ref[own, :, 0:1], turn_cols_ref[own, :, 1:2]
     left, right = result[:, :modes], result[:, modes:]
@@ -347,7 +396,7 @@
     out_cols = lax.broadcasted_iota(jnp.int32, (block, width), 1)
     pick = jnp.where(out_cols == out_rows // 2 + lax.rem(out_rows, 2) * modes, 1.0, 0.0)
     spread = jnp.where(rows == cols // 2 + lax.rem(cols, 2) * modes, 1.0, 0.0)
-    cov_ref[0] = exact(exact(pick, result), spread)
+    cov_ref[0] = spread_by(picked_by(pick, result), spread)
     means = lax.dot_general(
         jnp.broadcast_to(state, (8, width)), pick, (((1,), (1,)), ((), ())),
         precision=exact_mode, preferred_element_type=jnp.float32,
@@ -396,7 +445,6 @@
             pltpu.VMEM((steps, width, width), jnp.float32),
             pltpu.VMEM((steps, width, width), jnp.float32),
             pltpu.VMEM((2 * steps, 8, width), jnp.float32),
-            pltpu.VMEM((4, 2, width, width), jnp.bfloat16),
             pltpu.VMEM((max(1, steps // 2), width, width), jnp.float32),
         ],
         name="solve",

time: 29.2 us -> 25 us (0.86)
  Pallas kernels: 27.7 us -> 23.5 us
    pallas_call x1, Pallas kernels: 16.8 us -> 12.8 us  [local(): pl.pallas_call(functools.partial(solve_kernel, 'tm', 'rows'), out_shape=(...]
    pallas_call x1, Pallas kernels: 11 us -> 10.7 us  [local(): pl.pallas_call(functools.partial(share_kernel, 'tm'), out_shape=(jax.Shap...]
where the time goes in v2:
time: 25 us; the launch traced here: 24.8 us
  Pallas kernels  23.5 us (94%)
  between operations  1.28 us (5%)
    pallas_call x1, Pallas kernels, local(): pl.pallas_call(functools.partial(solve_kernel, 'tm', 'rows'), out_shape=(...  12.8 us
    pallas_call x1, Pallas kernels, local(): pl.pallas_call(functools.partial(share_kernel, 'tm'), out_shape=(jax.Shap...  10.7 us

profile of v2, /device:TPU:0, one launch (start us, length us, event | category | flops | bytes accessed | tf_op | source)
XLA Modules:
  0.0 24.8 jit_solution(11066470817780230976)
XLA Ops:
  1.3 10.7 %share.1 = (f32[8,8,256]{2,1,0:T(8,128)}, f32[8,8,128]{2,1,0:T(8,128)}, f32[8,128,8]{2,1,0:T(8,128)}, f32[8,128]{1,0:T(8,128)}, f32[128,8]{1,0:T(8,128)}) custom-call(s32[1]{0:T(128)S(6)} %copy.8.counts_ref, s32[1,2048]{1,0:T(1,128)} %site_ref.1, f32[1,2048]{1,0:T(1,128)} %obs_ref.1, f32[1,128]{1,0:T(1,128)} %bitcast.3, f32[1,128]{1,0:T(1,128)} %bitcast.4, ...), custom_call_target="tpu_custom_call" | custom-call | tf_op jit(solution)/shard_map/share/pallas_call | solution.py:415
  12.0 12.8 %solve.1 = (f32[1,64]{1,0:T(1,128)}, f32[1,64,256]{2,1,0:T(8,128)}) custom-call(f32[8,8,256]{2,1,0:T(8,128)} %get-tuple-element.7.sums_ref, f32[8,8,128]{2,1,0:T(8,128)} %get-tuple-element.8.turn_ref, f32[8,128,8]{2,1,0:T(8,128)} %get-tuple-element.9.turn_cols_ref, f32[8,128]{1,0:T(8,128)} %get-tuple-element.10.damp_ref, ...), custom_call_target="tpu_custom_call" | custom-call | tf_op jit(solution)/shard_map/solve/pallas_call | solution.py:435
